TPU v7x, 256 devices: a whole 4x4x8 slice. The times are simulated.
256 devices in a mesh: seq: 64 (over z, x, core), tp: 4 (over y).
Axes of the slice: x: 4, y: 4, z: 8, core: 2. Of those that a mesh axis runs over, the one named last changes fastest.
Arguments:
- tokens: bfloat16 [8192, 2048], P('seq'), may hold values from -6 to 6
- input_heads: bfloat16 [8192, 4096], P('seq', 'tp'), may hold values from -6 to 6
- z_gate: bfloat16 [8192, 4096], P('seq', 'tp'), may hold values from -6 to 6
- b_proj: bfloat16 [8192, 128], P('seq'), may hold values from -0.5 to 0.5
- c_proj: bfloat16 [8192, 128], P('seq'), may hold values from -0.5 to 0.5
- step_size: float32 [8192, 64], P('seq', 'tp'), may hold values from 0.5 to 2
- decay_log: float32 [8192, 64], P('seq', 'tp'), as said below
- skip_gain: float32 [64], P('tp'), may hold values from 0.5 to 2
- init_state: float32 [64, 64, 128], P('tp'), may hold values from -48 to 48
- norm_gain: float32 [4096], P('tp'), may hold values from 0.1 to 1.9
- out_weight: bfloat16 [4096, 2048], P('tp'), may hold values from -0.09375 to 0.09375
- moe_gain: float32 [2048], replicated, may hold values from 0.1 to 1.9
- routes: int32 [8192, 2], P('seq'), may hold values from 0 to 63, all different within a row; in each aligned block of 128 rows (0 to 127, 128 to 255, ...) at most 8 rows name the same one
- route_weights: float32 [8192, 2], P('seq'), may hold values from 0.2 to 1
- w_gate: bfloat16 [64, 2048, 2048], P('seq', None, 'tp'), may hold values from -0.125 to 0.125
- w_up: bfloat16 [64, 2048, 2048], P('seq', None, 'tp'), may hold values from -0.125 to 0.125
- w_down: bfloat16 [64, 2048, 2048], P('seq', 'tp'), may hold values from -0.125 to 0.125
Outputs:
- mixed_out: bfloat16 [8192, 2048], P('seq', 'tp')
Inputs may be any that keep to these rules, and one draw needn't show every extreme that they name: `decay_log`: every entry is negative. `routes`: the two experts of a row differ. In each aligned block of 128 rows (the rows of one device) no expert is named by more than 8 rows, a bound that some block reaches.
All inputs are finite; a program needn't handle non-finite values.
Results may differ from a plain program's by a relative error of at most 0.02.
Values may be sent and summed in bfloat16 or wider, within the bound.
A program may use at most 128 MiB of HBM per device.

v0:
```python
import jax
import jax.numpy as jnp
from jax import lax
from jax.sharding import PartitionSpec as P


def entering(part, axis, combine, identity):
    place = lax.axis_index(axis)
    gathered = jax.tree.map(lambda a: lax.all_gather(a, axis), part)
    state = jax.tree.map(lambda a, e: jnp.zeros_like(a) + jnp.asarray(e, a.dtype), part, identity)

    def one(turn, state):
        return combine(
            state, jax.tree.map(lambda a: lax.dynamic_index_in_dim(a, turn, 0, False), gathered)
        )

    return lax.fori_loop(0, place, one, state)


def rms_rows(values, scale_gain):
    wide_vals = values.astype(jnp.float32)
    mean_sq = jnp.mean(wide_vals * wide_vals, axis=-1, keepdims=True)
    return (wide_vals * lax.rsqrt(mean_sq + 1e-05) * scale_gain).astype(jnp.bfloat16)


def merge_carry(first_part, second_part):
    decay_first, state_first = first_part
    decay_second, state_second = second_part
    return (decay_first * decay_second, decay_second[:, None, None] * state_first + state_second)


def body(
    tokens,
    input_heads,
    z_gate,
    b_proj,
    c_proj,
    step_size,
    decay_log,
    skip_gain,
    init_state,
    norm_gain,
    out_weight,
    moe_gain,
    routes,
    route_weights,
    w_gate,
    w_up,
    w_down,
):
    highest = lax.Precision.HIGHEST
    tok_rows = input_heads.shape[0]
    head_count = step_size.shape[1]
    head_size = init_state.shape[1]
    x_wide = input_heads.astype(jnp.float32).reshape(tok_rows, head_count, head_size)
    input_matrix_broad = b_proj.astype(jnp.float32)
    c_wide = c_proj.astype(jnp.float32)
    cum_decay = jnp.cumsum(decay_log, axis=0)
    end_decay = cum_decay[-1]
    positions = jnp.arange(tok_rows, dtype=jnp.int32)
    causal = positions[:, None] >= positions[None, :]
    scores = jnp.einsum("in,jn->ij", c_proj, b_proj, preferred_element_type=jnp.float32)
    cum_heads = cum_decay.T
    log_gap = cum_heads[:, :, None] - cum_heads[:, None, :]
    decay_mat = jnp.where(causal, jnp.exp(jnp.where(causal, log_gap, 0.0)), 0.0)
    mix_weights = decay_mat * scores[None] * step_size.T[:, None, :]
    intra_part = jnp.einsum("hij,jhp->ihp", mix_weights, x_wide, precision=highest)
    weighted = (jnp.exp(end_decay[None, :] - cum_decay) * step_size)[:, :, None] * x_wide
    local_state = jnp.einsum("jhp,jn->hpn", weighted, input_matrix_broad, precision=highest)
    block_decay = jnp.exp(end_decay)
    prior_decay, prior_state = entering(
        (block_decay, local_state),
        "seq",
        merge_carry,
        (jnp.ones_like(block_decay), jnp.zeros_like(local_state)),
    )
    arriving_rows = prior_decay[:, None, None] * init_state + prior_state
    inter_part = (
        jnp.einsum("in,hpn->ihp", c_wide, arriving_rows, precision=highest)
        * jnp.exp(cum_decay)[:, :, None]
    )
    ssd_out = intra_part + inter_part + skip_gain[None, :, None] * x_wide
    z_wide = z_gate.astype(jnp.float32).reshape(tok_rows, head_count, head_size)
    gated_vals = ssd_out * jax.nn.silu(z_wide)
    gated_vals = gated_vals * lax.rsqrt(
        jnp.mean(gated_vals * gated_vals, axis=2, keepdims=True) + 1e-05
    )
    normed = (gated_vals.reshape(tok_rows, head_count * head_size) * norm_gain).astype(jnp.bfloat16)
    partial_value = jnp.dot(normed, out_weight, preferred_element_type=jnp.float32)
    model_width = out_weight.shape[1]
    width_share = model_width // lax.axis_size("tp")
    col_start = lax.axis_index("tp") * width_share
    seq_count = lax.axis_size("seq")
    expert_count = w_gate.shape[0] * seq_count
    slot_count = 4 * tok_rows // seq_count
    top_count = routes.shape[1]
    flat_expert = routes.reshape(-1)
    onehot = (flat_expert[:, None] == jnp.arange(expert_count, dtype=jnp.int32)[None, :]).astype(
        jnp.int32
    )
    earlier_count = jnp.cumsum(onehot, axis=0) - onehot
    slot_rank = jnp.sum(earlier_count * onehot, axis=1)
    placed = flat_expert * slot_count + slot_rank
    owners = jnp.arange(top_count * tok_rows, dtype=jnp.int32) // top_count
    source = jnp.full((expert_count * slot_count,), tok_rows, jnp.int32).at[placed].set(owners)
    proj_sum = lax.psum(partial_value.astype(jnp.bfloat16), "tp").astype(jnp.float32)
    hidden_full = (tokens.astype(jnp.float32) + proj_sum).astype(jnp.bfloat16)
    moe_in = rms_rows(hidden_full, moe_gain)
    outgoing = jnp.take(moe_in, source, axis=0, mode="fill", fill_value=0).reshape(
        expert_count, slot_count, model_width
    )
    hidden = lax.dynamic_slice_in_dim(hidden_full, col_start, width_share, 1)
    moe_rows = lax.all_to_all(outgoing, "seq", split_axis=0, concat_axis=0, tiled=True)
    src_count, item_count, full_width = moe_rows.shape
    flat_rows = moe_rows.reshape(src_count * item_count, full_width)
    gate_val = jnp.dot(flat_rows, w_gate[0], preferred_element_type=jnp.float32)
    up_val = jnp.dot(flat_rows, w_up[0], preferred_element_type=jnp.float32)
    act_vals = (jax.nn.silu(gate_val) * up_val).astype(jnp.bfloat16)
    down_val = jnp.dot(act_vals, w_down[0], preferred_element_type=jnp.float32)
    summed = lax.psum_scatter(down_val.astype(jnp.bfloat16), "tp", scatter_dimension=1, tiled=True)
    results = summed.reshape(src_count, item_count, -1)
    returned = lax.all_to_all(results, "seq", split_axis=0, concat_axis=0, tiled=True)
    chosen_indices = jnp.take(
        returned.reshape(expert_count * slot_count, width_share), placed, axis=0
    ).reshape(tok_rows, top_count, width_share)
    mixed_out = hidden.astype(jnp.float32) + jnp.sum(
        route_weights[:, :, None] * chosen_indices.astype(jnp.float32), axis=1
    )
    return mixed_out.astype(jnp.bfloat16)


def solution(mesh):
    in_specs = (
        P("seq", None),
        P("seq", "tp"),
        P("seq", "tp"),
        P("seq", None),
        P("seq", None),
        P("seq", "tp"),
        P("seq", "tp"),
        P("tp"),
        P("tp", None, None),
        P("tp"),
        P("tp", None),
        P(),
        P("seq", None),
        P("seq", None),
        P("seq", None, "tp"),
        P("seq", None, "tp"),
        P("seq", "tp", None),
    )
    out_specs = P("seq", "tp")
    return jax.shard_map(body, mesh=mesh, in_specs=in_specs, out_specs=out_specs, check_vma=False)
```

profile of v0, /device:TPU:1, one launch (start us, length us, event | category | flops | bytes accessed | tf_op | source)
XLA Modules:
  0.0 428.5 jit_solution(1268096922327915747)
XLA Ops:
  6.6 0.9 copy.54
  7.5 0.2 reduce_window_sum.26
  7.7 0.8 copy.58
  8.6 0.1 copy.59
  8.6 1.1 copy.57
  9.8 2.0 fusion.34
  11.8 0.1 copy.63
  11.9 0.1 eq.26
  12.0 0.1 reshape.134
  12.2 0.7 copy.55
  12.9 0.1 copy.61
  13.1 0.6 reduce-window.6
  13.7 0.2 slice_reduce_fusion
  13.9 0.1 copy.68
  14.1 0.1 mul.172
  14.2 0.1 fusion.49
  14.3 1.4 scatter_custom_fusion
  15.7 44.0 %all-gather.1 = f32[64,1,16]{2,1,0:T(1,128)S(1)} all-gather(f32[1,1,16]{2,1,0:T(1,128)S(1)} %get-tuple-element.60), channel_id=1, replica_groups=mesh['seq'=64,'tp'=4] {'seq'}, dimensions={0}, use_global_device_ids=true | all-gather | bytes 4160 | tf_op jit(solution)/shard_map/all_gather | solution.py:9
  59.8 0.6 iota_compare_fusion.2
  60.4 0.1 fusion.59
  60.5 97.7 %all-gather.4.cloned.1.call-done = f32[1024,64,128]{2,1,0:T(8,128)} async-done(((f32[16,64,128]{2,1,0:T(8,128)}), f32[1024,64,128]{2,1,0:T(8,128)}) %all-gather.4.cloned.1.call-update) | async-done | bytes 33554448 | tf_op jit(solution)/shard_map/all_gather | solution.py:9
  158.3 1.2 while.12
  158.3 1.2 bitcast_add_fusion.2
  159.5 1.5 fusion.20
  161.1 2.3 multiply_reduce_fusion.1
  163.5 0.2 fusion.35
  163.7 1.5 convolution_convert_fusion.1
  165.3 0.1 broadcast_in_dim.65
  165.4 117.4 %all-reduce.2.cloned.1.call-done = bf16[128,2048]{1,0:T(8,128)(2,1)} async-done(((bf16[128,2048]{1,0:T(8,128)(2,1)}), bf16[128,2048]{1,0:T(8,128)(2,1)}) %all-reduce.2.cloned.1.call-update) | async-done | bytes 524304 | tf_op jit(solution)/shard_map/psum | solution.py:106
  282.8 1.3 fusion.21
  284.1 0.2 fusion.23
  284.3 3.3 gather_fusion
  287.7 1.8 bitcast_select_fusion
  289.5 62.1 %all_to_all.10 = bf16[64,8,2048]{2,1,0:T(8,128)(2,1)S(1)} all-to-all(bf16[64,8,2048]{2,1,0:T(8,128)(2,1)S(1)} %bitcast_select_fusion), channel_id=1, replica_groups=mesh['seq'=64,'tp'=4] {'seq'}, dimensions={0} | all-to-all | bytes 4194304 | tf_op jit(solution)/shard_map/all_to_all | solution.py:113
  351.6 1.3 copy-done.2
  352.9 2.2 fusion.3
  355.1 6.3 %convolution_convert_fusion = bf16[512,2048]{1,0:T(8,128)(2,1)} fusion(bf16[1,512,2048]{2,1,0:T(8,128)(2,1)S(1)} %copy-done, bf16[1,2048,512]{2,1,0:T(8,128)(2,1)} %param.34, bf16[64,8,2048]{2,1,0:T(8,128)(2,1)} %copy-done.2, f32[512,512]{1,0:T(8,128)} %fusion.3), kind=kOutput, calls=%fused_computation.5 | convolution fusion | flops 2150105088 | bytes 9437184 | tf_op jit(solution)/shard_map/dot_general | solution.py:119
  361.4 29.5 %reduce-scatter.2.cloned.1.call-done = bf16[512,512]{1,0:T(8,128)(2,1)} async-done(((bf16[512,2048]{1,0:T(8,128)(2,1)}), bf16[512,512]{1,0:T(8,128)(2,1)}) %reduce-scatter.2.cloned.1.call-update) | async-done | bytes 524304 | tf_op jit(solution)/shard_map/reduce_scatter | solution.py:120
  390.9 10.6 %all-to-all-start.1 = ((bf16[64,8,512]{2,1,0:T(8,128)(2,1)}), bf16[64,8,512]{2,1,0:T(8,128)(2,1)S(1)}, u32[]{:S(2)}, u32[]{:S(2)}) async-start(bf16[64,8,512]{2,1,0:T(8,128)(2,1)} %bitcast.100), calls=%async_computation.2 | async-start | bytes 1048576 | tf_op jit(solution)/shard_map/all_to_all | solution.py:122
  401.5 0.1 reduce_sum.42
  401.6 0.1 copy.66
  401.7 0.1 copy.67
  401.9 0.1 copy.62
  402.0 17.2 %all-to-all-done.1 = bf16[64,8,512]{2,1,0:T(8,128)(2,1)S(1)} async-done(((bf16[64,8,512]{2,1,0:T(8,128)(2,1)}), bf16[64,8,512]{2,1,0:T(8,128)(2,1)S(1)}, u32[]{:S(2)}, u32[]{:S(2)}) %all-to-all-start.1) | async-done | bytes 524320 | tf_op jit(solution)/shard_map/all_to_all | solution.py:122
  419.2 1.2 gather_fusion.1
  420.3 0.1 gather.15
  420.4 0.8 multiply_reduce_fusion
  421.3 0.7 add_convert_fusion.1
  (59 shorter events, 0.6 us)
Async XLA Ops:
  6.5 348.6 %copy-start = (bf16[1,512,2048]{2,1,0:T(8,128)(2,1)S(1)}, bf16[1,512,2048]{2,1,0:T(8,128)(2,1)}, u32[]{:S(2)}) copy-start(bf16[1,512,2048]{2,1,0:T(8,128)(2,1)} %param.35) | copy-start | bytes 6291460
  6.5 53.8 %copy-start.5 = (bf16[128,128]{1,0:T(8,128)(2,1)S(1)}, bf16[128,128]{1,0:T(8,128)(2,1)}, u32[]{:S(2)}) copy-start(bf16[128,128]{1,0:T(8,128)(2,1)} %param.22) | copy-start | bytes 98308
  6.5 5.2 %copy-start.9 = (s32[128,2]{0,1:T(2,128)S(1)}, s32[128,2]{0,1:T(2,128)}, u32[]{:S(2)}) copy-start(s32[128,2]{0,1:T(2,128)} %param.31) | copy-start | bytes 3076
  6.5 6.4 %copy-start.4 = (bf16[128,1024]{1,0:T(8,128)(2,1)S(1)}, bf16[128,1024]{1,0:T(8,128)(2,1)}, u32[]{:S(2)}) copy-start(bf16[128,1024]{1,0:T(8,128)(2,1)} %param.21) | copy-start | bytes 786436
  6.5 53.8 %copy-start.6 = (bf16[128,128]{1,0:T(8,128)(2,1)S(1)}, bf16[128,128]{1,0:T(8,128)(2,1)}, u32[]{:S(2)}) copy-start(bf16[128,128]{1,0:T(8,128)(2,1)} %param.23) | copy-start | bytes 98308
  6.5 151.7 %all-gather.4.cloned.1.call-start = ((), (), s32[]{:S(2)}) async-start(), calls=%async_computation.5 | async-start | bytes 34078720 | tf_op jit(solution)/shard_map/all_gather | solution.py:9
  11.7 271.1 %all-reduce.2.cloned.1.call-start = ((), (), s32[]{:S(2)}) async-start(), calls=%async_computation.3 | async-start | bytes 1048576 | tf_op jit(solution)/shard_map/psum | solution.py:106
  14.3 45.4 %copy-start.7 = (s32[256]{0:T(256)}, s32[256]{0:T(256)S(1)}, u32[]{:S(2)}) copy-start(s32[256]{0:T(256)S(1)} %fusion.49) | copy-start | bytes 3076
  14.3 143.9 %copy-start.13 = (s32[256,1]{0,1:T(1,128)}, s32[256,1]{0,1:T(1,128)S(1)}, u32[]{:S(2)}) copy-start(s32[256,1]{0,1:T(1,128)S(1)} %compare_select_fusion) | copy-start | bytes 3076
  161.0 2.4 copy-start.12
  161.1 2.6 copy-start.1
  163.7 119.1 %copy-start.3 = (bf16[128,2048]{1,0:T(8,128)(2,1)S(1)}, bf16[128,2048]{1,0:T(8,128)(2,1)}, u32[]{:S(2)}) copy-start(bf16[128,2048]{1,0:T(8,128)(2,1)} %param.19) | copy-start | bytes 1572868
  165.2 118.9 %copy-start.11 = (f32[2048]{0:T(1024)S(1)}, f32[2048]{0:T(1024)}, u32[]{:S(2)}) copy-start(f32[2048]{0:T(1024)} %param.30) | copy-start | bytes 24580
  165.3 225.6 %reduce-scatter.2.cloned.1.call-start = ((), (), s32[]{:S(2)}) async-start(), calls=%async_computation.4 | async-start | bytes 2621440 | tf_op jit(solution)/shard_map/reduce_scatter | solution.py:120
  289.5 63.4 %copy-start.16 = (bf16[1,2048,512]{2,1,0:T(8,128)(2,1)S(1)}, bf16[1,2048,512]{2,1,0:T(8,128)(2,1)}, u32[]{:S(2)}) copy-start(bf16[1,2048,512]{2,1,0:T(8,128)(2,1)} %param.33) | copy-start | bytes 6291460
  351.6 1.3 copy-start.2
  361.4 40.1 %copy-start.8 = (s32[256]{0:T(256)S(1)}, s32[256]{0:T(256)}, u32[]{:S(2)}) copy-start(s32[256]{0:T(256)} %copy-done.7) | copy-start | bytes 3076
  361.4 40.3 %copy-start.10 = (s32[128,2]{0,1:T(2,128)S(1)}, s32[128,2]{0,1:T(2,128)}, u32[]{:S(2)}) copy-start(s32[128,2]{0,1:T(2,128)} %param.31) | copy-start | bytes 3076
  361.4 40.5 %copy-start.15 = (f32[128,2]{0,1:T(2,128)S(1)}, f32[128,2]{0,1:T(2,128)}, u32[]{:S(2)}) copy-start(f32[128,2]{0,1:T(2,128)} %param.32) | copy-start | bytes 3076
  361.4 40.6 %copy-start.14 = (s32[256,1]{0,1:T(1,128)S(1)}, s32[256,1]{0,1:T(1,128)}, u32[]{:S(2)}) copy-start(s32[256,1]{0,1:T(1,128)} %copy-done.13) | copy-start | bytes 3076
  390.9 28.3 %all-to-all-start.1 = ((bf16[64,8,512]{2,1,0:T(8,128)(2,1)}), bf16[64,8,512]{2,1,0:T(8,128)(2,1)S(1)}, u32[]{:S(2)}, u32[]{:S(2)}) async-start(bf16[64,8,512]{2,1,0:T(8,128)(2,1)} %bitcast.100), calls=%async_computation.2 | async-start | bytes 1048576 | tf_op jit(solution)/shard_map/all_to_all | solution.py:122
Sparse Core Ops, SparseCore 0:
  11.8 146.3 all-gather.3
  165.4 117.3 all-reduce.1
  361.5 29.3 reduce-scatter.1
where the time goes:
time: 432 us; the launch traced here: 429 us
  waiting for transfers between devices  262 us (61%)
  blocking collectives  106 us (25%)
  matrix products  15.9 us (4%)
  between operations  13.5 us (3%)
  local copies, waits for them, and re-layouts  12.6 us (3%)
  starting transfers between devices  10.7 us (2%)
  other arithmetic  7.94 us (2%)
    psum x1, waiting for transfers between devices, body(): lax.psum(partial_value.astype(jnp.bfloat16), 'tp').astype(jnp.float32)  117 us
    all_gather x1, waiting for transfers between devices, entering(): gathered = jax.tree.map(lambda a: lax.all_gather(a, axis), part)  97.7 us
    all_to_all x1, blocking collectives, body(): lax.all_to_all(outgoing, 'seq', split_axis=0, concat_axis=0, tiled=True)  62.1 us
    all_gather x1, blocking collectives, entering(): gathered = jax.tree.map(lambda a: lax.all_gather(a, axis), part)  44 us
    reduce_scatter x1, waiting for transfers between devices, body(): lax.psum_scatter(down_val.astype(jnp.bfloat16), 'tp', scatter_dimension=1...  29.5 us
    all_to_all x1, waiting for transfers between devices, body(): lax.all_to_all(results, 'seq', split_axis=0, concat_axis=0, tiled=True)  17.2 us
    all_to_all x1, starting transfers between devices, body(): lax.all_to_all(results, 'seq', split_axis=0, concat_axis=0, tiled=True)  10.6 us
  transfers between devices with their start and end apart: 4, of which 4 were waited for; matrix products, arithmetic and copies ran while one was open for 1% of the time, Pallas kernels for 0%

commit v1 on v0

--- a/solution.py
+++ b/solution.py
@@ -103,7 +103,8 @@
     placed = flat_expert * slot_count + slot_rank
     owners = jnp.arange(top_count * tok_rows, dtype=jnp.int32) // top_count
     source = jnp.full((expert_count * slot_count,), tok_rows, jnp.int32).at[placed].set(owners)
-    proj_sum = lax.psum(partial_value.astype(jnp.bfloat16), "tp").astype(jnp.float32)
+    _change_sources_all = lambda in_array: jnp.sum(lax.all_gather(in_array, "tp"), axis=0)
+    proj_sum = _change_sources_all(partial_value.astype(jnp.bfloat16)).astype(jnp.float32)
     hidden_full = (tokens.astype(jnp.float32) + proj_sum).astype(jnp.bfloat16)
     moe_in = rms_rows(hidden_full, moe_gain)
     outgoing = jnp.take(moe_in, source, axis=0, mode="fill", fill_value=0).reshape(

time: 432 us -> 419 us (0.970)
  waiting for transfers between devices: 262 us -> 248 us
    psum x1 -> x0, waiting for transfers between devices: 117 us -> none  [body(): lax.psum(partial_value.astype(jnp.bfloat16), 'tp').astype(jnp.float32)]
    all_gather x0 -> x1, waiting for transfers between devices: none -> 101 us  [body(): lax.all_gather(in_array, 'tp')]
where the time goes in v1:
time: 419 us; the launch traced here: 415 us
  waiting for transfers between devices  248 us (59%)
  blocking collectives  104 us (25%)
  matrix products  15.9 us (4%)
  between operations  13.4 us (3%)
  local copies, waits for them, and re-layouts  12.6 us (3%)
  starting transfers between devices  10.7 us (3%)
  other arithmetic  9.97 us (2%)
    all_gather x1, waiting for transfers between devices, body(): lax.all_gather(in_array, 'tp')  101 us
    all_gather x1, waiting for transfers between devices, entering(): gathered = jax.tree.map(lambda a: lax.all_gather(a, axis), part)  101 us
    all_to_all x1, blocking collectives, body(): lax.all_to_all(outgoing, 'seq', split_axis=0, concat_axis=0, tiled=True)  60.3 us
    all_gather x1, blocking collectives, entering(): gathered = jax.tree.map(lambda a: lax.all_gather(a, axis), part)  44 us
    reduce_scatter x1, waiting for transfers between devices, body(): lax.psum_scatter(down_val.astype(jnp.bfloat16), 'tp', scatter_dimension=1...  28.9 us
    all_to_all x1, waiting for transfers between devices, body(): lax.all_to_all(results, 'seq', split_axis=0, concat_axis=0, tiled=True)  17.2 us
    all_to_all x1, starting transfers between devices, body(): lax.all_to_all(results, 'seq', split_axis=0, concat_axis=0, tiled=True)  10.6 us
  transfers between devices with their start and end apart: 4, of which 4 were waited for; matrix products, arithmetic and copies ran while one was open for 1% of the time, Pallas kernels for 0%

profile of v1, /device:TPU:1, one launch (start us, length us, event | category | flops | bytes accessed | tf_op | source)
XLA Modules:
  0.0 415.4 jit_solution(14350686415505870814)
XLA Ops:
  6.6 1.0 copy.54
  7.6 0.2 reduce_window_sum.26
  7.7 0.8 copy.58
  8.6 1.1 copy.57
  9.8 1.9 fusion.34
  11.9 0.7 copy.55
  12.5 0.1 copy.61
  12.7 44.0 %all-gather.2 = f32[64,1,16]{2,1,0:T(1,128)S(1)} all-gather(f32[1,1,16]{2,1,0:T(1,128)S(1)} %get-tuple-element.60), channel_id=1, replica_groups=mesh['seq'=64,'tp'=4] {'seq'}, dimensions={0}, use_global_device_ids=true | all-gather | bytes 4160 | tf_op jit(solution)/shard_map/all_gather | solution.py:9
  56.7 0.6 iota_compare_fusion.2
  57.3 0.1 fusion.59
  57.4 100.8 %all-gather.6.cloned.1.call-done = f32[1024,64,128]{2,1,0:T(8,128)} async-done(((f32[16,64,128]{2,1,0:T(8,128)}), f32[1024,64,128]{2,1,0:T(8,128)}) %all-gather.6.cloned.1.call-update) | async-done | bytes 33554448 | tf_op jit(solution)/shard_map/all_gather | solution.py:9
  158.3 1.2 while.12
  158.4 1.2 bitcast_add_fusion.2
  159.6 1.5 fusion.20
  161.1 2.3 multiply_reduce_fusion.1
  163.5 0.2 fusion.35
  163.8 1.5 convolution_convert_fusion.1
  165.4 0.1 copy.63
  165.5 0.1 eq.26
  165.6 0.1 reshape.134
  165.8 0.6 reduce-window.6
  166.4 0.2 slice_reduce_fusion
  166.6 0.1 copy.68
  166.8 0.1 mul.172
  166.9 0.1 fusion.49
  167.0 1.4 scatter_custom_fusion
  168.5 0.1 broadcast_in_dim.65
  168.6 101.5 %all-gather.8.cloned.1.call-done = bf16[512,2048]{1,0:T(8,128)(2,1)} async-done(((bf16[128,2048]{1,0:T(8,128)(2,1)}), bf16[512,2048]{1,0:T(8,128)(2,1)}) %all-gather.8.cloned.1.call-update) | async-done | bytes 2097168 | tf_op jit(solution)/shard_map/all_gather | solution.py:106
  270.0 2.0 reduce_sum.53
  272.1 1.3 fusion.21
  273.4 0.2 fusion.23
  273.6 3.3 gather_fusion
  277.0 1.8 bitcast_select_fusion
  278.8 60.3 %all_to_all.10 = bf16[64,8,2048]{2,1,0:T(8,128)(2,1)S(1)} all-to-all(bf16[64,8,2048]{2,1,0:T(8,128)(2,1)S(1)} %bitcast_select_fusion), channel_id=1, replica_groups=mesh['seq'=64,'tp'=4] {'seq'}, dimensions={0} | all-to-all | bytes 4194304 | tf_op jit(solution)/shard_map/all_to_all | solution.py:114
  339.0 1.3 copy-done.2
  340.3 2.2 fusion.3
  342.6 6.3 %convolution_convert_fusion = bf16[512,2048]{1,0:T(8,128)(2,1)} fusion(bf16[1,512,2048]{2,1,0:T(8,128)(2,1)S(1)} %copy-done, bf16[1,2048,512]{2,1,0:T(8,128)(2,1)} %param.34, bf16[64,8,2048]{2,1,0:T(8,128)(2,1)} %copy-done.2, f32[512,512]{1,0:T(8,128)} %fusion.3), kind=kOutput, calls=%fused_computation.5 | convolution fusion | flops 2150105088 | bytes 9437184 | tf_op jit(solution)/shard_map/dot_general | solution.py:120
  348.9 28.9 %reduce-scatter.2.cloned.1.call-done = bf16[512,512]{1,0:T(8,128)(2,1)} async-done(((bf16[512,2048]{1,0:T(8,128)(2,1)}), bf16[512,512]{1,0:T(8,128)(2,1)}) %reduce-scatter.2.cloned.1.call-update) | async-done | bytes 524304 | tf_op jit(solution)/shard_map/reduce_scatter | solution.py:121
  377.7 10.6 %all-to-all-start.1 = ((bf16[64,8,512]{2,1,0:T(8,128)(2,1)}), bf16[64,8,512]{2,1,0:T(8,128)(2,1)S(1)}, u32[]{:S(2)}, u32[]{:S(2)}) async-start(bf16[64,8,512]{2,1,0:T(8,128)(2,1)} %bitcast.102), calls=%async_computation.2 | async-start | bytes 1048576 | tf_op jit(solution)/shard_map/all_to_all | solution.py:123
  388.3 0.1 reduce_sum.55
  388.5 0.1 copy.66
  388.6 0.1 copy.67
  388.7 0.1 copy.62
  388.8 17.2 %all-to-all-done.1 = bf16[64,8,512]{2,1,0:T(8,128)(2,1)S(1)} async-done(((bf16[64,8,512]{2,1,0:T(8,128)(2,1)}), bf16[64,8,512]{2,1,0:T(8,128)(2,1)S(1)}, u32[]{:S(2)}, u32[]{:S(2)}) %all-to-all-start.1) | async-done | bytes 524320 | tf_op jit(solution)/shard_map/all_to_all | solution.py:123
  406.0 1.2 gather_fusion.1
  407.2 0.1 gather.15
  407.3 0.8 multiply_reduce_fusion
  408.2 0.7 add_convert_fusion.1
  (50 shorter events, 0.6 us)
Async XLA Ops:
  6.5 336.0 %copy-start = (bf16[1,512,2048]{2,1,0:T(8,128)(2,1)S(1)}, bf16[1,512,2048]{2,1,0:T(8,128)(2,1)}, u32[]{:S(2)}) copy-start(bf16[1,512,2048]{2,1,0:T(8,128)(2,1)} %param.35) | copy-start | bytes 6291460
  6.5 50.8 %copy-start.4 = (bf16[128,128]{1,0:T(8,128)(2,1)S(1)}, bf16[128,128]{1,0:T(8,128)(2,1)}, u32[]{:S(2)}) copy-start(bf16[128,128]{1,0:T(8,128)(2,1)} %param.22) | copy-start | bytes 98308
  6.5 6.0 %copy-start.3 = (bf16[128,1024]{1,0:T(8,128)(2,1)S(1)}, bf16[128,1024]{1,0:T(8,128)(2,1)}, u32[]{:S(2)}) copy-start(bf16[128,1024]{1,0:T(8,128)(2,1)} %param.21) | copy-start | bytes 786436
  6.5 50.8 %copy-start.5 = (bf16[128,128]{1,0:T(8,128)(2,1)S(1)}, bf16[128,128]{1,0:T(8,128)(2,1)}, u32[]{:S(2)}) copy-start(bf16[128,128]{1,0:T(8,128)(2,1)} %param.23) | copy-start | bytes 98308
  6.5 151.7 %all-gather.6.cloned.1.call-start = ((), (), s32[]{:S(2)}) async-start(), calls=%async_computation.4 | async-start | bytes 34078720 | tf_op jit(solution)/shard_map/all_gather | solution.py:9
  11.7 258.3 %all-gather.8.cloned.1.call-start = ((), (), s32[]{:S(2)}) async-start(), calls=%async_computation.5 | async-start | bytes 2621440 | tf_op jit(solution)/shard_map/all_gather | solution.py:106
  158.3 2.8 copy-start.11
  161.1 2.4 copy-start.8
  161.1 2.6 copy-start.1
  163.8 1.6 copy-start.6
  165.3 212.4 %reduce-scatter.2.cloned.1.call-start = ((), (), s32[]{:S(2)}) async-start(), calls=%async_computation.3 | async-start | bytes 2621440 | tf_op jit(solution)/shard_map/reduce_scatter | solution.py:121
  270.0 3.4 copy-start.7
  278.8 61.6 %copy-start.10 = (bf16[1,2048,512]{2,1,0:T(8,128)(2,1)S(1)}, bf16[1,2048,512]{2,1,0:T(8,128)(2,1)}, u32[]{:S(2)}) copy-start(bf16[1,2048,512]{2,1,0:T(8,128)(2,1)} %param.33) | copy-start | bytes 6291460
  339.0 1.3 copy-start.2
  348.8 39.9 %copy-start.9 = (f32[128,2]{0,1:T(2,128)S(1)}, f32[128,2]{0,1:T(2,128)}, u32[]{:S(2)}) copy-start(f32[128,2]{0,1:T(2,128)} %param.32) | copy-start | bytes 3076
  377.7 28.3 %all-to-all-start.1 = ((bf16[64,8,512]{2,1,0:T(8,128)(2,1)}), bf16[64,8,512]{2,1,0:T(8,128)(2,1)S(1)}, u32[]{:S(2)}, u32[]{:S(2)}) async-start(bf16[64,8,512]{2,1,0:T(8,128)(2,1)} %bitcast.102), calls=%async_computation.2 | async-start | bytes 1048576 | tf_op jit(solution)/shard_map/all_to_all | solution.py:123
Sparse Core Ops, SparseCore 0:
  11.9 146.3 all-gather.5
  165.5 104.5 all-gather.7
  349.0 28.6 reduce-scatter.1
